TPU v7x, 256 devices: a whole 4x4x8 slice. The times are simulated.
256 devices in a mesh: blk: 32 (over x_hi, z, core), req: 8 (over y, x_lo).
Axes of the slice: x: 4 (x_hi: 2, x_lo: 2; x = x_hi * 2 + x_lo), y: 4, z: 8, core: 2. Of those that a mesh axis runs over, the one named last changes fastest.
Arguments:
- prefill_queries: bfloat16 [8, 512, 1024], P('req', 'blk'), may hold values from -6 to 6
- decode_queries: bfloat16 [128, 1024], P('req'), may hold values from -6 to 6
- new_prefill: bfloat16 [8, 512, 512], P('req', 'blk'), may hold values from -6 to 6
- new_decode: bfloat16 [128, 512], P('req'), may hold values from -6 to 6
- prefill_cache: bfloat16 [8, 4096, 512], P('req', 'blk'), may hold values from -5 to 5
- decode_cache: bfloat16 [128, 4096, 512], P('req', 'blk'), may hold values from -5 to 5
- prefill_offsets: int32 [8], P('req'), may hold values from 2 to 3584, as said below
- decode_lengths: int32 [128], P('req'), may hold values from 2 to 4095, as said below
- dealing: int32 [136], replicated, may hold values from 0 to 127, as said below
Outputs:
- prefill_out: bfloat16 [8, 512, 1024], P('req', 'blk')
- decode_out: bfloat16 [128, 1024], P('req')
- prefill_cache_out: bfloat16 [8, 4096, 512], P('req', 'blk')
- decode_cache_out: bfloat16 [128, 4096, 512], P('req', 'blk')
Inputs may be any that keep to these rules, and one draw needn't show every extreme that they name: The block of prefill slot i fills positions prefill_offsets[i] to prefill_offsets[i] + 511; some slot has offset 4096 - 512. The new token of decode slot j goes to position decode_lengths[j]; some slot has length 4095. `dealing`: the first 8 entries are a permutation of 0 to 7, the other 128 a permutation of 0 to 127.
All inputs are finite; a program needn't handle non-finite values.
Results may differ from a plain program's by a relative error of at most 0.0085.
Values may be sent and summed in bfloat16 or wider, within the bound.
A program may use at most 64 MiB of HBM per device.

v0:
```python
import jax
import jax.numpy as jnp
from jax import lax
from jax.sharding import PartitionSpec as P

QUERY_HEADS = 8
KEY_VALUE_HEADS = 2
HEAD_SIZE = 128
masked_fill = -1e30


def merged(part, axis, combine):
    gathered = jax.tree.map(lambda a: lax.all_gather(a, axis), part)

    def take(source):
        return jax.tree.map(lambda a: lax.dynamic_index_in_dim(a, source, 0, False), gathered)

    return lax.fori_loop(
        1, lax.axis_size(axis), lambda source, state: combine(state, take(source)), take(0)
    )


def write_block(cache_table, block_rows, offsets, positions):
    piece_len = block_rows.shape[1]
    relative = positions[None, :] - offsets[:, None]
    picked = jax.vmap(lambda source_rows, row_index: source_rows[row_index])(
        block_rows, jnp.clip(relative, 0, piece_len - 1)
    )
    inside = (relative >= 0) & (relative < piece_len)
    return jnp.where(inside[:, :, None], picked, cache_table)


def scores_of(query_rows, cache_table, limits, key_pos):
    slot_total, row_total = (query_rows.shape[0], query_rows.shape[1])
    column_total = cache_table.shape[1]
    grouped_queries = query_rows.reshape(
        slot_total, row_total, KEY_VALUE_HEADS, QUERY_HEADS // KEY_VALUE_HEADS, HEAD_SIZE
    )
    key_portion = cache_table[:, :, : KEY_VALUE_HEADS * HEAD_SIZE].reshape(
        slot_total, column_total, KEY_VALUE_HEADS, HEAD_SIZE
    )
    scores = jnp.einsum(
        "nrgqd,ncgd->ngqrc", grouped_queries, key_portion, preferred_element_type=jnp.float32
    ) * HEAD_SIZE ** (-0.5)
    visible = (key_pos[None, None, :] <= limits[:, :, None])[:, None, None]
    return (jnp.where(visible, scores, masked_fill), visible)


def weigh_values(scores, visible, maxima, cache_table):
    slot_total, column_total = (cache_table.shape[0], cache_table.shape[1])
    exponent = jnp.where(visible, jnp.exp(scores - maxima[..., None]), 0.0)
    value_portion = cache_table[:, :, KEY_VALUE_HEADS * HEAD_SIZE :].reshape(
        slot_total, column_total, KEY_VALUE_HEADS, HEAD_SIZE
    )
    weighted = jnp.einsum(
        "ngqrc,ncgd->ngqrd",
        exponent.astype(jnp.bfloat16),
        value_portion,
        preferred_element_type=jnp.float32,
    )
    return (jnp.sum(exponent, axis=-1), weighted)


def finish_rows(totals, weighted):
    normed = weighted / totals[..., None]
    slot_total, row_total = (normed.shape[0], normed.shape[3])
    return (
        jnp.transpose(normed, (0, 3, 1, 2, 4))
        .reshape(slot_total, row_total, QUERY_HEADS * HEAD_SIZE)
        .astype(jnp.bfloat16)
    )


def combine(first, second):
    first_max, first_total, first_sum = first
    second_max, second_total, second_sum = second
    joined = jnp.maximum(first_max, second_max)
    first_scale = jnp.exp(first_max - joined)
    second_scale = jnp.exp(second_max - joined)
    return (
        joined,
        first_total * first_scale + second_total * second_scale,
        first_sum * first_scale[..., None] + second_sum * second_scale[..., None],
    )


def per_device(
    prefill_queries,
    decode_queries,
    new_prefill,
    new_decode,
    prefill_cache,
    decode_cache,
    prefill_offsets,
    decode_lengths,
    dealing,
):
    ctx_dev = prefill_cache.shape[1]
    blk_index = lax.axis_index("blk")
    positions = blk_index * ctx_dev + jnp.arange(ctx_dev, dtype=jnp.int32)
    written = positions[None, :] == decode_lengths[:, None]
    decode_cache_out = jnp.where(written[:, :, None], new_decode[:, None, :], decode_cache)
    dec_scores, dec_visible = scores_of(
        decode_queries[:, None, :], decode_cache_out, decode_lengths[:, None], positions
    )
    dec_max = jnp.max(dec_scores, axis=-1)
    dec_total, dec_sum = weigh_values(dec_scores, dec_visible, dec_max, decode_cache_out)
    dec_max, dec_total, dec_sum = merged((dec_max, dec_total, dec_sum), "blk", combine)
    decode_attn = finish_rows(dec_total, dec_sum)[:, 0, :]
    block_rows, whole_queries = (
        lax.all_gather(new_prefill, "blk", axis=1, tiled=True),
        lax.all_gather(prefill_queries, "blk", axis=1, tiled=True),
    )
    prefill_cache_out = write_block(prefill_cache, block_rows, prefill_offsets, positions)
    limits = prefill_offsets[:, None] + jnp.arange(whole_queries.shape[1], dtype=jnp.int32)[None, :]
    scores, visible = scores_of(whole_queries, prefill_cache_out, limits, positions)
    maxima = jnp.max(scores, axis=-1)
    totals, weighted = weigh_values(scores, visible, maxima, prefill_cache_out)
    peer_max, peer_total, peer_sum = (
        lax.all_to_all(maxima[None], "blk", split_axis=4, concat_axis=0, tiled=True),
        lax.all_to_all(totals[None], "blk", split_axis=4, concat_axis=0, tiled=True),
        lax.all_to_all(weighted[None], "blk", split_axis=4, concat_axis=0, tiled=True),
    )
    joined = jnp.max(peer_max, axis=0)
    peer_scale = jnp.exp(peer_max - joined[None])
    totals = jnp.sum(peer_total * peer_scale, axis=0)
    weighted = jnp.sum(peer_sum * peer_scale[..., None], axis=0)
    prefill_attn = finish_rows(totals, weighted)
    gathered_pre, gathered_dec = (
        lax.all_gather(prefill_attn, "req", axis=0, tiled=True),
        lax.all_gather(decode_attn, "req", axis=0, tiled=True),
    )
    group_index = lax.axis_index("req")
    pre_count = prefill_attn.shape[0]
    dec_count = decode_attn.shape[0]
    total_pre = gathered_pre.shape[0]
    own_pre = group_index * pre_count + jnp.arange(pre_count, dtype=jnp.int32)
    own_dec = group_index * dec_count + jnp.arange(dec_count, dtype=jnp.int32)
    pre_selector = (dealing[:total_pre][None, :] == own_pre[:, None]).astype(jnp.bfloat16)
    dec_selector = (dealing[total_pre:][None, :] == own_dec[:, None]).astype(jnp.bfloat16)
    prefill_out = jnp.einsum(
        "rs,sbf->rbf", pre_selector, gathered_pre, preferred_element_type=jnp.float32
    ).astype(jnp.bfloat16)
    decode_out = jnp.dot(dec_selector, gathered_dec, preferred_element_type=jnp.float32).astype(
        jnp.bfloat16
    )
    return (prefill_out, decode_out, prefill_cache_out, decode_cache_out)


def solution(mesh):
    in_specs = (
        P("req", "blk", None),
        P("req", None),
        P("req", "blk", None),
        P("req", None),
        P("req", "blk", None),
        P("req", "blk", None),
        P("req"),
        P("req"),
        P(),
    )
    out_specs = (
        P("req", "blk", None),
        P("req", None),
        P("req", "blk", None),
        P("req", "blk", None),
    )
    return jax.shard_map(
        per_device, mesh=mesh, in_specs=in_specs, out_specs=out_specs, check_vma=False
    )
```

profile of v0, /device:TPU:6, one launch (start us, length us, event | category | flops | bytes accessed | tf_op | source)
XLA Modules:
  0.0 344.9 jit_solution(14435808164075506)
XLA Ops:
  8.0 3.9 %copy.83 = bf16[16,128,512]{1,2,0:T(8,128)(2,1)} copy(bf16[16,128,512]{2,1,0:T(8,128)(2,1)} %param.16) | data formatting | bytes 4194304 | tf_op args[5]
  12.0 2.5 broadcast_select_fusion
  15.1 1.3 fusion.28
  16.5 2.6 copy.95
  19.8 44.6 %all_gather.30 = bf16[1,512,512]{2,1,0:T(8,128)(2,1)S(1)} all-gather(bf16[1,16,512]{2,1,0:T(8,128)(2,1)S(1)} %copy-done.4), channel_id=1, replica_groups=mesh['blk'=32,'req'=8] {'blk'}, dimensions={1}, use_global_device_ids=true | all-gather | bytes 540672 | tf_op jit(solution)/shard_map/all_gather | solution.py:111
  64.4 1.2 gather_fusion
  65.9 38.4 %all-gather = f32[512,2,4]{2,1,0:T(2,128)S(1)} all-gather(f32[16,2,4]{2,1,0:T(2,128)S(1)} %get-tuple-element.249), channel_id=2, replica_groups=mesh['blk'=32,'req'=8] {'blk'}, dimensions={0}, use_global_device_ids=true | all-gather | bytes 16896 | tf_op jit(solution)/shard_map/all_gather | solution.py:13
  104.6 39.6 %all-gather.1 = f32[512,2,4]{2,1,0:T(2,128)S(1)} all-gather(f32[16,2,4]{2,1,0:T(2,128)S(1)} %fusion.26), channel_id=3, replica_groups=mesh['blk'=32,'req'=8] {'blk'}, dimensions={0}, use_global_device_ids=true | all-gather | bytes 16896 | tf_op jit(solution)/shard_map/all_gather | solution.py:13
  144.3 1.1 copy.91
  145.4 1.1 copy.92
  146.8 1.5 copy.70
  149.1 1.4 reshape.386
  150.5 5.5 %all-to-all-start.1 = ((f32[32,1,128]{2,1,0:T(1,128)}), f32[32,1,128]{2,1,0:T(1,128)S(1)}, u32[]{:S(2)}, u32[]{:S(2)}) async-start(f32[32,1,128]{2,1,0:T(1,128)} %reshape.386), calls=%async_computation.1 | async-start | bytes 32768 | tf_op jit(solution)/shard_map/all_to_all | solution.py:120
  156.8 1.4 reshape.388
  158.2 4.9 %all-to-all-done.1 = f32[32,1,128]{2,1,0:T(1,128)S(1)} async-done(((f32[32,1,128]{2,1,0:T(1,128)}), f32[32,1,128]{2,1,0:T(1,128)S(1)}, u32[]{:S(2)}, u32[]{:S(2)}) %all-to-all-start.1) | async-done | bytes 16416 | tf_op jit(solution)/shard_map/all_to_all | solution.py:120
  163.1 6.7 %all-to-all-start.2 = ((f32[32,1,128]{2,1,0:T(1,128)}), f32[32,1,128]{2,1,0:T(1,128)S(1)}, u32[]{:S(2)}, u32[]{:S(2)}) async-start(f32[32,1,128]{2,1,0:T(1,128)} %reshape.388), calls=%async_computation.2 | async-start | bytes 32768 | tf_op jit(solution)/shard_map/all_to_all | solution.py:121
  170.5 2.6 copy.76
  175.8 1.0 all-to-all-done.2
  176.8 8.8 %all-to-all-start = ((f32[1,1,2,4,512,128]{5,3,2,1,0,4:T(4,128)}), f32[1,1,2,4,512,128]{5,3,2,1,0,4:T(4,128)S(1)}, u32[]{:S(2)}, u32[]{:S(2)}) async-start(f32[1,1,2,4,512,128]{5,3,2,1,0,4:T(4,128)} %copy.76), calls=%async_computation | async-start | bytes 4194304 | tf_op jit(solution)/shard_map/all_to_all | solution.py:122
  188.7 88.2 %while.19 = (s32[]{:T(128)}, f32[16,2,4,1]{0,2,3,1:T(4,128)S(1)}, f32[16,2,4,1]{0,2,3,1:T(4,128)S(1)}, f32[16,2,4,1,128]{4,3,2,1,0:T(1,128)S(1)}, f32[32,16,2,4,...) while((s32[]{:T(128)}, f32[16,2,4,1]{0,2,3,1:T(4,128)S(1)}, ...), condition=%wide.region_8.9_spmd, body=%wide.region_7.8_spmd.sunk | while | flops 50053 | bytes 337563 | solution.py:18
  190.1 0.9 constant_dynamic-slice_fusion.2
  192.9 0.9 constant_dynamic-slice_fusion.2
  195.8 0.9 constant_dynamic-slice_fusion.2
  198.6 0.9 constant_dynamic-slice_fusion.2
  204.3 0.9 constant_dynamic-slice_fusion.2
  210.0 0.9 constant_dynamic-slice_fusion.2
  215.7 0.9 constant_dynamic-slice_fusion.2
  227.2 0.9 constant_dynamic-slice_fusion.2
  230.0 0.9 constant_dynamic-slice_fusion.2
  247.1 0.9 constant_dynamic-slice_fusion.2
  277.4 29.2 %all_gather.39 = bf16[128,1024]{1,0:T(8,128)(2,1)S(1)} all-gather(bf16[16,1024]{1,0:T(8,128)(2,1)S(1)} %convert_element_type.51), channel_id=1, replica_groups=mesh['blk'=32,'req'=8] {'req'}, dimensions={0}, use_global_device_ids=true | all-gather | bytes 294912 | tf_op jit(solution)/shard_map/all_gather | solution.py:131
  308.2 28.9 %all_gather.32 = bf16[8,16,1024]{2,1,0:T(8,128)(2,1)S(1)} all-gather(bf16[1,16,1024]{2,1,0:T(8,128)(2,1)S(1)} %convert_element_type.46), channel_id=1, replica_groups=mesh['blk'=32,'req'=8] {'req'}, dimensions={0}, use_global_device_ids=true | all-gather | bytes 294912 | tf_op jit(solution)/shard_map/all_gather | solution.py:130
  (276 shorter events, 92.5 us)
Async XLA Ops:
  7.2 139.6 %all-gather.6.cloned.1.call-start = ((), (), s32[]{:S(2)}) async-start(), calls=%async_computation.3 | async-start | bytes 1081344 | tf_op jit(solution)/shard_map/all_gather | solution.py:112
  7.9 179.9 %all-gather.8.cloned.1.call-start = ((), (), s32[]{:S(2)}) async-start(), calls=%async_computation.4 | async-start | bytes 2162688 | tf_op jit(solution)/shard_map/all_gather | solution.py:13
  8.0 4.0 %copy-start.2 = (bf16[16,1024]{1,0:T(8,128)(2,1)S(1)}, bf16[16,1024]{1,0:T(8,128)(2,1)}, u32[]{:S(2)}) copy-start(bf16[16,1024]{1,0:T(8,128)(2,1)} %param.12) | copy-start | bytes 98308
  8.0 4.0 %copy-start.6 = (s32[16]{0:T(128)S(1)}, s32[16]{0:T(128)}, u32[]{:S(2)}) copy-start(s32[16]{0:T(128)} %param.18) | copy-start | bytes 196
  8.0 4.1 %copy-start.3 = (bf16[16,512]{1,0:T(8,128)(2,1)S(1)}, bf16[16,512]{1,0:T(8,128)(2,1)}, u32[]{:S(2)}) copy-start(bf16[16,512]{1,0:T(8,128)(2,1)} %param.14) | copy-start | bytes 49156
  16.5 3.3 copy-start.4
  16.5 49.1 %copy-start.1 = (bf16[1,128,512]{2,1,0:T(8,128)(2,1)S(1)}, bf16[1,128,512]{2,1,0:T(8,128)(2,1)}, u32[]{:S(2)}) copy-start(bf16[1,128,512]{2,1,0:T(8,128)(2,1)} %param.15) | copy-start | bytes 393220
  64.4 82.2 %copy-start.5 = (s32[136]{0:T(256)S(1)}, s32[136]{0:T(256)}, u32[]{:S(2)}) copy-start(s32[136]{0:T(256)} %param.19) | copy-start | bytes 1636
  65.7 82.6 %copy-start = (bf16[1,128,512]{2,1,0:T(8,128)(2,1)}, bf16[1,128,512]{2,1,0:T(8,128)(2,1)S(1)}, u32[]{:S(2)}) copy-start(bf16[1,128,512]{2,1,0:T(8,128)(2,1)S(1)} %bitcast_select_fusion.1) | copy-start | bytes 393220
  150.5 12.6 %all-to-all-start.1 = ((f32[32,1,128]{2,1,0:T(1,128)}), f32[32,1,128]{2,1,0:T(1,128)S(1)}, u32[]{:S(2)}, u32[]{:S(2)}) async-start(f32[32,1,128]{2,1,0:T(1,128)} %reshape.386), calls=%async_computation.1 | async-start | bytes 32768 | tf_op jit(solution)/shard_map/all_to_all | solution.py:120
  163.1 13.7 %all-to-all-start.2 = ((f32[32,1,128]{2,1,0:T(1,128)}), f32[32,1,128]{2,1,0:T(1,128)S(1)}, u32[]{:S(2)}, u32[]{:S(2)}) async-start(f32[32,1,128]{2,1,0:T(1,128)} %reshape.388), calls=%async_computation.2 | async-start | bytes 32768 | tf_op jit(solution)/shard_map/all_to_all | solution.py:121
  176.8 130.6 %all-to-all-start = ((f32[1,1,2,4,512,128]{5,3,2,1,0,4:T(4,128)}), f32[1,1,2,4,512,128]{5,3,2,1,0,4:T(4,128)S(1)}, u32[]{:S(2)}, u32[]{:S(2)}) async-start(f32[1,1,2,4,512,128]{5,3,2,1,0,4:T(4,128)} %copy.76), calls=%async_computation | async-start | bytes 4194304 | tf_op jit(solution)/shard_map/all_to_all | solution.py:122
Sparse Core Ops, SparseCore 0:
  10.8 79.0 all-gather.5
  92.7 76.8 all-gather.7
where the time goes:
time: 349 us; the launch traced here: 345 us
  blocking collectives  181 us (52%)
  other arithmetic  61.4 us (18%)
  local copies, waits for them, and re-layouts  55.1 us (16%)
  starting transfers between devices  21.1 us (6%)
  between operations  15 us (4%)
  waiting for transfers between devices  6.66 us (2%)
  matrix products  4.23 us (1%)
    all_gather x2, blocking collectives, merged(): gathered = jax.tree.map(lambda a: lax.all_gather(a, axis), part)  77.9 us
    all_gather x1, blocking collectives, per_device(): lax.all_gather(new_prefill, 'blk', axis=1, tiled=True)  44.6 us
    all_gather x1, blocking collectives, per_device(): lax.all_gather(decode_attn, 'req', axis=0, tiled=True)  29.2 us
    all_gather x1, blocking collectives, per_device(): lax.all_gather(prefill_attn, 'req', axis=0, tiled=True)  28.9 us
    dynamic_slice x36, local copies, waits for them, and re-layouts, take(): lax.dynamic_index_in_dim(a, source, 0, False)  27.4 us
    mul x31, other arithmetic, combine(): second_sum * second_scale[..., None]  21.9 us
    mul x31, other arithmetic, combine(): first_sum * first_scale[..., None] + second_sum * second_scale[..., None]  21.4 us
    add x31, other arithmetic, combine(): first_sum * first_scale[..., None] + second_sum * second_scale[..., None]  12 us
  transfers between devices with their start and end apart: 5, of which 2 were waited for; matrix products, arithmetic and copies ran while one was open for 34% of the time, Pallas kernels for 0%

commit v1 on v0

--- a/solution.py
+++ b/solution.py
@@ -108,7 +108,9 @@
     dec_max, dec_total, dec_sum = merged((dec_max, dec_total, dec_sum), "blk", combine)
     decode_attn = finish_rows(dec_total, dec_sum)[:, 0, :]
     block_rows, whole_queries = (
-        lax.all_gather(new_prefill, "blk", axis=1, tiled=True),
+        jnp.concatenate(
+            lax.all_to_all(jnp.stack([new_prefill] * lax.axis_size("blk")), "blk", 0, 0), axis=1
+        ),
         lax.all_gather(prefill_queries, "blk", axis=1, tiled=True),
     )
     prefill_cache_out = write_block(prefill_cache, block_rows, prefill_offsets, positions)

time: 349 us -> 337 us (0.966)
  blocking collectives: 181 us -> 140 us
  waiting for transfers between devices: 6.66 us -> 19.6 us
  starting transfers between devices: 21.1 us -> 33.3 us
    all_gather x1 -> x0, blocking collectives: 44.6 us -> none  [per_device(): lax.all_gather(new_prefill, 'blk', axis=1, tiled=True)]
    all_gather x1, waiting for transfers between devices: 0.02 us -> 13 us  [merged(): gathered = jax.tree.map(lambda a: lax.all_gather(a, axis), part)]
    all_to_all x0 -> x1, starting transfers between devices: none -> 11.6 us  [per_device(): lax.all_to_all(jnp.stack([new_prefill] * lax.axis_size('blk')), 'blk', 0, 0)]
    all_gather x2, blocking collectives: 77.9 us -> 82.4 us  [merged(): gathered = jax.tree.map(lambda a: lax.all_gather(a, axis), part)]
  transfers between devices with their start and end apart: 5 -> 6, of which waited for: 2 -> 3; matrix products, arithmetic and copies ran while one was open for 34% -> 36% of each run, Pallas kernels for 0% -> 0%
where the time goes in v1:
time: 337 us; the launch traced here: 331 us
  blocking collectives  140 us (42%)
  other arithmetic  61.4 us (18%)
  local copies, waits for them, and re-layouts  56 us (17%)
  starting transfers between devices  33.3 us (10%)
  waiting for transfers between devices  19.6 us (6%)
  between operations  15.1 us (4%)
  matrix products  4.23 us (1%)
    all_gather x2, blocking collectives, merged(): gathered = jax.tree.map(lambda a: lax.all_gather(a, axis), part)  82.4 us
    all_gather x1, blocking collectives, per_device(): lax.all_gather(prefill_attn, 'req', axis=0, tiled=True)  29 us
    all_gather x1, blocking collectives, per_device(): lax.all_gather(decode_attn, 'req', axis=0, tiled=True)  28.9 us
    dynamic_slice x36, local copies, waits for them, and re-layouts, take(): lax.dynamic_index_in_dim(a, source, 0, False)  27.4 us
    mul x31, other arithmetic, combine(): second_sum * second_scale[..., None]  21.9 us
    mul x31, other arithmetic, combine(): first_sum * first_scale[..., None] + second_sum * second_scale[..., None]  21.4 us
    all_gather x1, waiting for transfers between devices, merged(): gathered = jax.tree.map(lambda a: lax.all_gather(a, axis), part)  13 us
    add x31, other arithmetic, combine(): first_sum * first_scale[..., None] + second_sum * second_scale[..., None]  12 us
  transfers between devices with their start and end apart: 6, of which 3 were waited for; matrix products, arithmetic and copies ran while one was open for 36% of the time, Pallas kernels for 0%

profile of v1, /device:TPU:6, one launch (start us, length us, event | category | flops | bytes accessed | tf_op | source)
XLA Modules:
  0.0 330.6 jit_solution(3615379111863960665)
XLA Ops:
  8.0 3.9 %copy.83 = bf16[16,128,512]{1,2,0:T(8,128)(2,1)} copy(bf16[16,128,512]{2,1,0:T(8,128)(2,1)} %param.16) | data formatting | bytes 4194304 | tf_op args[5]
  12.0 2.5 broadcast_select_fusion
  15.1 1.3 fusion.28
  17.3 11.6 %all-to-all-start = ((bf16[32,1,16,512]{3,2,1,0:T(8,128)(2,1)}), bf16[32,1,16,512]{3,2,1,0:T(8,128)(2,1)S(1)}, u32[]{:S(2)}, u32[]{:S(2)}) async-start(bf16[32,1,16,512]{3,2,1,0:T(8,128)(2,1)} %stack.2), calls=%async_computation | async-start | bytes 1048576 | tf_op jit(solution)/shard_map/all_to_all | solution.py:112
  28.9 2.6 copy.95
  32.2 44.1 %all-gather = f32[512,2,4]{2,1,0:T(2,128)S(1)} all-gather(f32[16,2,4]{2,1,0:T(2,128)S(1)} %get-tuple-element.249), channel_id=2, replica_groups=mesh['blk'=32,'req'=8] {'blk'}, dimensions={0}, use_global_device_ids=true | all-gather | bytes 16896 | tf_op jit(solution)/shard_map/all_gather | solution.py:13
  76.6 38.3 %all-gather.1 = f32[512,2,4]{2,1,0:T(2,128)S(1)} all-gather(f32[16,2,4]{2,1,0:T(2,128)S(1)} %fusion.26), channel_id=3, replica_groups=mesh['blk'=32,'req'=8] {'blk'}, dimensions={0}, use_global_device_ids=true | all-gather | bytes 16896 | tf_op jit(solution)/shard_map/all_gather | solution.py:13
  115.0 1.1 copy.91
  116.1 1.1 copy.92
  117.5 1.2 gather_fusion
  119.1 1.5 copy.70
  121.4 1.4 reshape.393
  122.8 6.1 %all-to-all-start.2 = ((f32[32,1,128]{2,1,0:T(1,128)}), f32[32,1,128]{2,1,0:T(1,128)S(1)}, u32[]{:S(2)}, u32[]{:S(2)}) async-start(f32[32,1,128]{2,1,0:T(1,128)} %reshape.393), calls=%async_computation.2 | async-start | bytes 32768 | tf_op jit(solution)/shard_map/all_to_all | solution.py:122
  129.8 1.4 reshape.395
  131.1 4.9 %all-to-all-done.2 = f32[32,1,128]{2,1,0:T(1,128)S(1)} async-done(((f32[32,1,128]{2,1,0:T(1,128)}), f32[32,1,128]{2,1,0:T(1,128)S(1)}, u32[]{:S(2)}, u32[]{:S(2)}) %all-to-all-start.2) | async-done | bytes 16416 | tf_op jit(solution)/shard_map/all_to_all | solution.py:122
  136.0 6.7 %all-to-all-start.3 = ((f32[32,1,128]{2,1,0:T(1,128)}), f32[32,1,128]{2,1,0:T(1,128)S(1)}, u32[]{:S(2)}, u32[]{:S(2)}) async-start(f32[32,1,128]{2,1,0:T(1,128)} %reshape.395), calls=%async_computation.3 | async-start | bytes 32768 | tf_op jit(solution)/shard_map/all_to_all | solution.py:123
  143.4 2.6 copy.76
  148.7 1.1 all-to-all-done.3
  149.7 8.8 %all-to-all-start.1 = ((f32[1,1,2,4,512,128]{5,3,2,1,0,4:T(4,128)}), f32[1,1,2,4,512,128]{5,3,2,1,0,4:T(4,128)S(1)}, u32[]{:S(2)}, u32[]{:S(2)}) async-start(f32[1,1,2,4,512,128]{5,3,2,1,0,4:T(4,128)} %copy.76), calls=%async_computation.1 | async-start | bytes 4194304 | tf_op jit(solution)/shard_map/all_to_all | solution.py:124
  160.7 13.0 %all-gather.8.cloned.1.call-done = f32[512,2,4,128]{3,2,1,0:T(4,128)} async-done(((f32[16,2,4,128]{3,2,1,0:T(4,128)}), f32[512,2,4,128]{3,2,1,0:T(4,128)}) %all-gather.8.cloned.1.call-update) | async-done | bytes 2097168 | tf_op jit(solution)/shard_map/all_gather | solution.py:13
  174.6 88.2 %while.19 = (s32[]{:T(128)}, f32[16,2,4,1]{0,2,3,1:T(4,128)S(1)}, f32[16,2,4,1]{0,2,3,1:T(4,128)S(1)}, f32[16,2,4,1,128]{4,3,2,1,0:T(1,128)S(1)}, f32[32,16,2,4,...) while((s32[]{:T(128)}, f32[16,2,4,1]{0,2,3,1:T(4,128)S(1)}, ...), condition=%wide.region_8.9_spmd, body=%wide.region_7.8_spmd.sunk | while | flops 50053 | bytes 337563 | solution.py:18
  176.0 0.9 constant_dynamic-slice_fusion.2
  178.8 0.9 constant_dynamic-slice_fusion.2
  187.3 0.9 constant_dynamic-slice_fusion.2
  190.2 0.9 constant_dynamic-slice_fusion.2
  193.0 0.9 constant_dynamic-slice_fusion.2
  195.9 0.9 constant_dynamic-slice_fusion.2
  201.6 0.9 constant_dynamic-slice_fusion.2
  207.3 0.9 constant_dynamic-slice_fusion.2
  210.1 0.9 constant_dynamic-slice_fusion.2
  263.2 28.9 %all_gather.35 = bf16[128,1024]{1,0:T(8,128)(2,1)S(1)} all-gather(bf16[16,1024]{1,0:T(8,128)(2,1)S(1)} %convert_element_type.51), channel_id=1, replica_groups=mesh['blk'=32,'req'=8] {'req'}, dimensions={0}, use_global_device_ids=true | all-gather | bytes 294912 | tf_op jit(solution)/shard_map/all_gather | solution.py:133
  293.8 29.0 %all_gather.28 = bf16[8,16,1024]{2,1,0:T(8,128)(2,1)S(1)} all-gather(bf16[1,16,1024]{2,1,0:T(8,128)(2,1)S(1)} %convert_element_type.46), channel_id=1, replica_groups=mesh['blk'=32,'req'=8] {'req'}, dimensions={0}, use_global_device_ids=true | all-gather | bytes 294912 | tf_op jit(solution)/shard_map/all_gather | solution.py:132
  (278 shorter events, 94.2 us)
Async XLA Ops:
  7.2 111.9 %all-gather.6.cloned.1.call-start = ((), (), s32[]{:S(2)}) async-start(), calls=%async_computation.4 | async-start | bytes 1081344 | tf_op jit(solution)/shard_map/all_gather | solution.py:114
  7.9 165.8 %all-gather.8.cloned.1.call-start = ((), (), s32[]{:S(2)}) async-start(), calls=%async_computation.5 | async-start | bytes 2162688 | tf_op jit(solution)/shard_map/all_gather | solution.py:13
  8.0 4.0 %copy-start.2 = (bf16[16,1024]{1,0:T(8,128)(2,1)S(1)}, bf16[16,1024]{1,0:T(8,128)(2,1)}, u32[]{:S(2)}) copy-start(bf16[16,1024]{1,0:T(8,128)(2,1)} %param.12) | copy-start | bytes 98308
  8.0 4.0 %copy-start.6 = (s32[16]{0:T(128)S(1)}, s32[16]{0:T(128)}, u32[]{:S(2)}) copy-start(s32[16]{0:T(128)} %param.18) | copy-start | bytes 196
  8.0 4.1 %copy-start.3 = (bf16[16,512]{1,0:T(8,128)(2,1)S(1)}, bf16[16,512]{1,0:T(8,128)(2,1)}, u32[]{:S(2)}) copy-start(bf16[16,512]{1,0:T(8,128)(2,1)} %param.14) | copy-start | bytes 49156
  14.7 1.8 copy-start.4
  17.3 100.2 %all-to-all-start = ((bf16[32,1,16,512]{3,2,1,0:T(8,128)(2,1)}), bf16[32,1,16,512]{3,2,1,0:T(8,128)(2,1)S(1)}, u32[]{:S(2)}, u32[]{:S(2)}) async-start(bf16[32,1,16,512]{3,2,1,0:T(8,128)(2,1)} %stack.2), calls=%async_computation | async-start | bytes 1048576 | tf_op jit(solution)/shard_map/all_to_all | solution.py:112
  31.5 85.7 %copy-start.5 = (s32[136]{0:T(256)S(1)}, s32[136]{0:T(256)}, u32[]{:S(2)}) copy-start(s32[136]{0:T(256)} %param.19) | copy-start | bytes 1636
  31.5 87.1 %copy-start.1 = (bf16[1,128,512]{2,1,0:T(8,128)(2,1)S(1)}, bf16[1,128,512]{2,1,0:T(8,128)(2,1)}, u32[]{:S(2)}) copy-start(bf16[1,128,512]{2,1,0:T(8,128)(2,1)} %param.15) | copy-start | bytes 393220
  118.8 2.4 copy-start
  122.8 13.2 %all-to-all-start.2 = ((f32[32,1,128]{2,1,0:T(1,128)}), f32[32,1,128]{2,1,0:T(1,128)S(1)}, u32[]{:S(2)}, u32[]{:S(2)}) async-start(f32[32,1,128]{2,1,0:T(1,128)} %reshape.393), calls=%async_computation.2 | async-start | bytes 32768 | tf_op jit(solution)/shard_map/all_to_all | solution.py:122
  136.0 13.7 %all-to-all-start.3 = ((f32[32,1,128]{2,1,0:T(1,128)}), f32[32,1,128]{2,1,0:T(1,128)S(1)}, u32[]{:S(2)}, u32[]{:S(2)}) async-start(f32[32,1,128]{2,1,0:T(1,128)} %reshape.395), calls=%async_computation.3 | async-start | bytes 32768 | tf_op jit(solution)/shard_map/all_to_all | solution.py:123
  149.7 143.2 %all-to-all-start.1 = ((f32[1,1,2,4,512,128]{5,3,2,1,0,4:T(4,128)}), f32[1,1,2,4,512,128]{5,3,2,1,0,4:T(4,128)S(1)}, u32[]{:S(2)}, u32[]{:S(2)}) async-start(f32[1,1,2,4,512,128]{5,3,2,1,0,4:T(4,128)} %copy.76), calls=%async_computation.1 | async-start | bytes 4194304 | tf_op jit(solution)/shard_map/all_to_all | solution.py:124
Sparse Core Ops, SparseCore 0:
  10.8 79.4 all-gather.5
  93.0 80.6 all-gather.7
